TPU v7x, 128 devices: a whole 4x4x4 slice. The times are simulated.
128 devices in a mesh: bins: 16 (over y, z), chan: 8 (over x, core).
Axes of the slice: x: 4, y: 4, z: 4, core: 2. Of those that a mesh axis runs over, the one named last changes fastest.
Arguments:
- tokens_in: bfloat16 [8192, 2048], P('bins', 'chan'), may hold values from -6 to 6
- filters: bfloat16 [8192, 2048], P('bins', 'chan'), may hold values from -0.0625 to 0.0625
- gate: bfloat16 [8192, 2048], P('bins', 'chan'), may hold values from -6 to 6
- skip: float32 [2048], P('chan'), may hold values from 0.5 to 1.5
- out_grad: bfloat16 [8192, 4096], P('bins', 'chan'), may hold values from -6 to 6
- out_weight: bfloat16 [2048, 4096], P('chan'), may hold values from -0.09375 to 0.09375
- owner: int32 [16, 512], P(None, 'bins'), may hold values from 0 to 15, as said below
- slot: int32 [16, 512], P(None, 'bins'), may hold values from 0 to 1023, as said below
Outputs:
- gate_grad: bfloat16 [16, 512, 2048], P(None, 'bins', 'chan')
- filter_grad: float32 [16, 512, 2048], P(None, 'bins', 'chan')
- grad_rows: bfloat16 [16384, 2048], P('bins', 'chan')
Inputs may be any that keep to these rules, and one draw needn't show every extreme that they name: Let the column group j be the entries [i, r] with j * 32 <= r < (j + 1) * 32, all i. Within one column group at most 64 entries name the same owner, and in every draw some owner is named exactly 64 times by every column group. An entry of column group j (as for owner) lies in j * 64 to (j + 1) * 64 - 1; no two tokens share an owner and a slot; in every draw some owner has all 1024 slots used.
All inputs are finite; a program needn't handle non-finite values.
Results may differ from a plain program's by a relative error of at most 0.012.
Values may be sent and summed in bfloat16 or wider, within the bound.
A program may use at most 128 MiB of HBM per device.

v0:
```python
import math
import jax
import jax.numpy as jnp
from jax import lax
from jax.sharding import PartitionSpec as P

exact_mode = lax.Precision.HIGHEST


def angles(index, period):
    return 2.0 * math.pi / period * (index % period).astype(jnp.float32)


def contract(table, values, form):
    return jnp.einsum(form, table, values, precision=exact_mode)


def product(left_re, left_im, right_re, right_im):
    return (left_re * right_re - left_im * right_im, left_re * right_im + left_im * right_re)


def shards(tokens_in, filters, gate, skip, out_grad, out_weight, owner, slot):
    blocks = lax.axis_size("bins")
    my_index = lax.axis_index("bins")
    tok_rows, channels = tokens_in.shape
    col_rows = tok_rows // blocks
    length = 2 * blocks * tok_rows
    block_ids = jnp.arange(blocks, dtype=jnp.int32)
    bin_order = jnp.stack(
        [block_ids, jnp.where(block_ids == 0, blocks, 2 * blocks - block_ids)], axis=1
    ).reshape(2 * blocks)
    block_angle = angles(bin_order[:, None] * block_ids[None, :], 2 * blocks)
    block_cos = jnp.cos(block_angle)
    block_sin = jnp.sin(block_angle)
    back_cos = block_cos.T
    back_sin = block_sin.T
    column_ids = my_index * col_rows + jnp.arange(col_rows, dtype=jnp.int32)
    ahead_angle = angles(bin_order[:, None] * column_ids[None, :], length)[:, :, None]
    ahead_cos = jnp.cos(ahead_angle)
    ahead_sin = jnp.sin(ahead_angle)
    own_bins = lax.dynamic_slice_in_dim(bin_order, 2 * my_index, 2)
    positions = jnp.arange(tok_rows, dtype=jnp.int32)
    return_angle = angles(own_bins[:, None] * positions[None, :], length)[:, :, None]
    return_cos = jnp.cos(return_angle)
    return_sin = jnp.sin(return_angle)
    inner_angle = angles(positions[:, None] * positions[None, :], tok_rows)
    inner_cos = jnp.cos(inner_angle)
    inner_sin = jnp.sin(inner_angle)
    upstream = lax.dot_general(
        lax.all_gather(out_grad, "chan", axis=1, tiled=True),
        out_weight,
        (((1,), (1,)), ((), ())),
        preferred_element_type=jnp.float32,
    )
    g_rounded = upstream.astype(jnp.bfloat16)
    grad_in = (g_rounded.astype(jnp.float32) * gate.astype(jnp.float32)).astype(jnp.bfloat16)
    grid_shape = (blocks, col_rows, channels)
    tok_cols, filt_cols, grad_cols, gout_cols = (
        lax.all_to_all(
            tokens_in.reshape(grid_shape), "bins", split_axis=0, concat_axis=0, tiled=True
        ),
        lax.all_to_all(
            filters.reshape(grid_shape), "bins", split_axis=0, concat_axis=0, tiled=True
        ),
        lax.all_to_all(
            grad_in.reshape(grid_shape), "bins", split_axis=0, concat_axis=0, tiled=True
        ),
        lax.all_to_all(
            g_rounded.reshape(grid_shape), "bins", split_axis=0, concat_axis=0, tiled=True
        ),
    )
    tok_real = tok_cols.astype(jnp.float32)
    filt_real = filt_cols.astype(jnp.float32)
    grad_real = grad_cols.astype(jnp.float32)
    real_stack = jnp.stack([tok_real, filt_real, grad_real])
    part_re = contract(block_cos, real_stack, "ki,sirc->skrc")
    part_im = -contract(block_sin, real_stack, "ki,sirc->skrc")
    turned = jnp.stack(
        [part_re * ahead_cos + part_im * ahead_sin, part_im * ahead_cos - part_re * ahead_sin],
        axis=1,
    )
    arrived = lax.all_to_all(turned, "bins", split_axis=2, concat_axis=3, tiled=True)
    came_re = arrived[:, 0]
    came_im = arrived[:, 1]
    spec_re = contract(inner_cos, came_re, "kr,slrc->slkc") + contract(
        inner_sin, came_im, "kr,slrc->slkc"
    )
    spec_im = contract(inner_cos, came_im, "kr,slrc->slkc") - contract(
        inner_sin, came_re, "kr,slrc->slkc"
    )
    spec_re, spec_im = (spec_re, spec_im)
    x_re, x_im = (spec_re[0], spec_im[0])
    h_re, h_im = (spec_re[1], spec_im[1])
    y_re, y_im = (spec_re[2], spec_im[2])
    conv_re, conv_im = product(x_re, x_im, h_re, h_im)
    back_re, back_im = product(h_re, -h_im, y_re, y_im)
    lag_re, lag_im = product(y_re, y_im, x_re, -x_im)
    freq_re = jnp.stack([conv_re, back_re, lag_re])
    freq_im = jnp.stack([conv_im, back_im, lag_im])
    sum_re = contract(inner_cos, freq_re, "rk,slkc->slrc") - contract(
        inner_sin, freq_im, "rk,slkc->slrc"
    )
    sum_im = contract(inner_cos, freq_im, "rk,slkc->slrc") + contract(
        inner_sin, freq_re, "rk,slkc->slrc"
    )
    twist_re = sum_re * return_cos - sum_im * return_sin
    twist_im = sum_re * return_sin + sum_im * return_cos
    turned = jnp.stack([twist_re, twist_im], axis=1)
    arrived = lax.all_to_all(turned, "bins", split_axis=3, concat_axis=2, tiled=True)
    came_re = arrived[:, 0]
    came_im = arrived[:, 1]
    out_re = contract(back_cos, came_re, "ik,skrc->sirc") - contract(
        back_sin, came_im, "ik,skrc->sirc"
    )
    result_re = out_re / length
    conv = result_re[0]
    backward = result_re[1]
    lagged = result_re[2]
    gate_grad = (gout_cols.astype(jnp.float32) * (conv + skip * tok_real)).astype(jnp.bfloat16)
    filter_grad = lagged / math.sqrt(blocks * tok_rows)
    token_grad = (backward + skip * grad_real).astype(jnp.bfloat16)
    send_rows = 2 * tok_rows // blocks
    targets = owner.reshape(-1) * send_rows + slot.reshape(-1) - my_index * send_rows
    outbox = (
        jnp.zeros((blocks * send_rows, channels), jnp.bfloat16)
        .at[targets]
        .set(token_grad.reshape(tok_rows, channels))
    )
    inbox = lax.all_to_all(
        outbox.reshape(blocks, send_rows, channels), "bins", split_axis=0, concat_axis=0, tiled=True
    )
    grad_rows = inbox.reshape(blocks * send_rows, channels)
    return (gate_grad, filter_grad, grad_rows)


def solution(mesh):
    return jax.shard_map(
        shards,
        mesh=mesh,
        in_specs=(
            P("bins", "chan"),
            P("bins", "chan"),
            P("bins", "chan"),
            P("chan"),
            P("bins", "chan"),
            P("chan", None),
            P(None, "bins"),
            P(None, "bins"),
        ),
        out_specs=(P(None, "bins", "chan"), P(None, "bins", "chan"), P("bins", "chan")),
        check_vma=False,
    )
```

profile of v0, /device:TPU:0, one launch (start us, length us, event | category | flops | bytes accessed | tf_op | source)
XLA Modules:
  0.0 452.5 jit_solution(11163061509946371895)
XLA Ops:
  7.2 0.0 copy-start
  7.2 0.0 all-gather.2.cloned.1.call-start
  7.2 0.7 all-gather.2.cloned.1.call-update
  7.9 8.2 %all-to-all-start.1 = ((bf16[16,32,256]{2,1,0:T(8,128)(2,1)}), bf16[16,32,256]{2,1,0:T(8,128)(2,1)S(1)}, u32[]{:S(2)}, u32[]{:S(2)}) async-start(bf16[16,32,256]{2,1,0:T(8,128)(2,1)} %bitcast.142), calls=%async_computation.1 | async-start | bytes 524288 | tf_op jit(solution)/shard_map/all_to_all | solution.py:59
  16.2 0.1 copy.47
  16.2 0.1 mul.319
  16.3 0.2 fusion.61
  16.5 8.1 %all-to-all-done.1 = bf16[16,32,256]{2,1,0:T(8,128)(2,1)S(1)} async-done(((bf16[16,32,256]{2,1,0:T(8,128)(2,1)}), bf16[16,32,256]{2,1,0:T(8,128)(2,1)S(1)}, u32[]{:S(2)}, u32[]{:S(2)}) %all-to-all-start.1) | async-done | bytes 262176 | tf_op jit(solution)/shard_map/all_to_all | solution.py:59
  24.6 3.6 all-to-all-start.2
  28.2 16.0 %all-gather.2.cloned.1.call-done = bf16[512,4096]{1,0:T(8,128)(2,1)} async-done(((bf16[512,512]{1,0:T(8,128)(2,1)}), bf16[512,4096]{1,0:T(8,128)(2,1)}) %all-gather.2.cloned.1.call-update) | async-done | bytes 4194320 | tf_op jit(solution)/shard_map/all_gather | solution.py:50
  44.2 0.0 copy-done
  44.2 4.3 multiply_convert_fusion
  48.5 0.0 all-to-all-done.2
  48.5 7.2 %all-to-all-start.3 = ((bf16[16,32,256]{2,1,0:T(8,128)(2,1)}), bf16[16,32,256]{2,1,0:T(8,128)(2,1)S(1)}, u32[]{:S(2)}, u32[]{:S(2)}) async-start(bf16[16,32,256]{2,1,0:T(8,128)(2,1)} %bitcast.5), calls=%async_computation.3 | async-start | bytes 524288 | tf_op jit(solution)/shard_map/all_to_all | solution.py:65
  55.7 0.2 convert_bitcast_fusion.1
  55.8 0.2 bitcast_convert_fusion
  56.0 8.6 %all-to-all-done.3 = bf16[16,32,256]{2,1,0:T(8,128)(2,1)S(1)} async-done(((bf16[16,32,256]{2,1,0:T(8,128)(2,1)}), bf16[16,32,256]{2,1,0:T(8,128)(2,1)S(1)}, u32[]{:S(2)}, u32[]{:S(2)}) %all-to-all-start.3) | async-done | bytes 262176 | tf_op jit(solution)/shard_map/all_to_all | solution.py:65
  64.6 0.2 convert_bitcast_fusion
  64.7 2.8 fusion.16
  67.5 3.6 fusion.3
  71.1 1.1 pad_maximum_fusion
  72.3 6.3 %copy.48 = f32[3,2,32,32,256]{4,3,0,1,2:T(8,128)} copy(f32[3,2,32,32,256]{4,2,3,0,1:T(8,128)S(1)} %pad_maximum_fusion) | data formatting | bytes 12582912 | tf_op jit(solution)/shard_map/stack | solution.py:78
  78.5 4.9 %all-to-all-start.4 = ((f32[3,2,32,32,256]{4,3,0,1,2:T(8,128)}), f32[3,2,32,32,256]{4,3,0,1,2:T(8,128)}, u32[]{:S(2)}, u32[]{:S(2)}) async-start(f32[3,2,32,32,256]{4,3,0,1,2:T(8,128)} %copy.48), calls=%async_computation.4 | async-start | bytes 12582912 | tf_op jit(solution)/shard_map/all_to_all | solution.py:82
  83.4 0.1 dynamic_slice.3
  83.5 0.2 fusion.75
  83.6 97.4 %all-to-all-done.4 = f32[3,2,32,32,256]{4,3,0,1,2:T(8,128)} async-done(((f32[3,2,32,32,256]{4,3,0,1,2:T(8,128)}), f32[3,2,32,32,256]{4,3,0,1,2:T(8,128)}, u32[]{:S(2)}, u32[]{:S(2)}) %all-to-all-start.4) | async-done | bytes 6291488 | tf_op jit(solution)/shard_map/all_to_all | solution.py:82
  181.1 3.5 copy.50
  184.6 14.7 %fusion.7 = f32[3,2,256,512]{3,2,1,0:T(8,128)S(1)} fusion(f32[3,2,2,512,256]{4,3,2,1,0:T(8,128)S(1)} %bitcast.136), kind=kOutput, calls=%fused_computation.24 | convolution fusion | flops 4835508224 | bytes 6291456 | tf_op jit(solution)/shard_map/kr,slrc->slkc/dot_general | solution.py:15
  199.3 14.5 %fusion.6 = f32[3,2,256,512]{3,2,1,0:T(8,128)S(1)} fusion(f32[3,2,2,512,256]{4,3,2,1,0:T(8,128)S(1)} %bitcast.137), kind=kOutput, calls=%fused_computation.23 | convolution fusion | flops 4835508224 | bytes 6291456 | tf_op jit(solution)/shard_map/kr,slrc->slkc/dot_general | solution.py:15
  213.8 14.6 %add_bitcast_fusion.1 = f32[3,2,512,256]{2,3,1,0:T(8,128)S(1)} fusion(f32[3,2,256,512]{3,2,1,0:T(8,128)S(1)} %fusion.7, f32[3,2,2,512,256]{4,3,2,1,0:T(8,128)S(1)} %bitcast.138), kind=kOutput, calls=%fused_computation.22 | convolution fusion | flops 4836294656 | bytes 9437184 | tf_op jit(solution)/shard_map/kr,slrc->slkc/dot_general | solution.py:15
  228.4 14.5 %subtract_bitcast_fusion.1 = f32[3,2,512,256]{2,3,1,0:T(8,128)S(1)} fusion(f32[3,2,256,512]{3,2,1,0:T(8,128)S(1)} %fusion.6, f32[3,2,2,512,256]{4,3,2,1,0:T(8,128)S(1)} %bitcast.139), kind=kOutput, calls=%fused_computation.21 | convolution fusion | flops 4836294656 | bytes 9437184 | tf_op jit(solution)/shard_map/kr,slrc->slkc/dot_general | solution.py:15
  242.9 0.8 multiply_subtract_fusion.1
  243.7 0.8 multiply_subtract_fusion.2
  244.5 9.5 %fusion.10 = f32[3,2,256,512]{3,2,1,0:T(8,128)S(1)} fusion(f32[1,2,512,256]{2,3,1,0:T(8,128)S(1)} %get-tuple-element.22, f32[1,2,512,256]{2,3,1,0:T(8,128)S(1)} %get-tuple-element.21, f32[1,2,512,256]{2,3,1,0:T(8,128)S(1)} %get-tuple-element.24), kind=kOutput, calls=%fused_computation.27 | convolution fusion | flops 4837081088 | bytes 6291456 | tf_op jit(solution)/shard_map/rk,slkc->slrc/dot_general | solution.py:15
  254.0 9.4 %fusion.11 = f32[3,2,256,512]{3,2,1,0:T(8,128)S(1)} fusion(f32[1,2,512,256]{2,3,1,0:T(8,128)S(1)} %get-tuple-element.22, f32[1,2,512,256]{2,3,1,0:T(8,128)S(1)} %get-tuple-element.21, f32[1,2,512,256]{2,3,1,0:T(8,128)S(1)} %get-tuple-element.24), kind=kOutput, calls=%fused_computation.28 | convolution fusion | flops 4837081088 | bytes 6291456 | tf_op jit(solution)/shard_map/rk,slkc->slrc/dot_general | solution.py:15
  263.4 9.8 %fusion.14 = f32[3,2,256,512]{3,2,1,0:T(8,128)S(1)} fusion(f32[3,2,256,512]{3,2,1,0:T(8,128)S(1)} %fusion.11, f32[1,2,512,256]{2,3,1,0:T(8,128)S(1)} %get-tuple-element.20, f32[1,2,512,256]{2,3,1,0:T(8,128)S(1)} %get-tuple-element.23, f32[1,2,512,256]{2,3,1,0:T(8,128)S(1)} %get-tuple-element.19), kind=kOutput, calls=%fused_computation.31 | convolution fusion | flops 4837867520 | bytes 9437184 | tf_op jit(solution)/shard_map/rk,slkc->slrc/dot_general | solution.py:15
  273.2 9.9 %subtract_bitcast_fusion = (f32[3,1,2,512,256]{3,4,2,0,1:T(8,128)S(1)}, f32[3,1,2,512,256]{3,4,2,0,1:T(8,128)S(1)}) fusion(f32[3,2,256,512]{3,2,1,0:T(8,128)S(1)} %fusion.14, f32[2,512]{1,0:T(2,128)S(1)} %get-tuple-element.30, f32[2,512]{1,0:T(2,128)S(1)} %get-tuple-element.29, f32[3,2,256,512]{3,2,1,0:T(8,128)S(1)} %fusion.10, ...), kind=kOutput, calls=%fused_computation.20 | convolution fusion | flops 4842586112 | bytes 15736832 | tf_op jit(solution)/shard_map/rk,slkc->slrc/dot_general | solution.py:15
  283.1 3.5 pad_maximum_fusion.1
  286.7 10.5 %copy.53 = f32[3,2,2,512,256]{4,2,0,1,3:T(2,128)} copy(f32[3,2,2,512,256]{3,4,2,0,1:T(8,128)} %pad_maximum_fusion.1) | data formatting | bytes 12582912 | tf_op jit(solution)/shard_map/stack | solution.py:108
  297.1 0.0 copy-start.2
  297.1 9.0 %all-to-all-start.5 = ((f32[3,2,2,512,256]{4,2,0,1,3:T(2,128)}), f32[3,2,2,512,256]{4,2,0,1,3:T(2,128)}, u32[]{:S(2)}, u32[]{:S(2)}) async-start(f32[3,2,2,512,256]{4,2,0,1,3:T(2,128)} %copy.53), calls=%async_computation.5 | async-start | bytes 12582912 | tf_op jit(solution)/shard_map/all_to_all | solution.py:109
  306.2 0.0 copy-done.2
  306.2 0.0 copy-done.3
  306.2 0.1 sub.74
  306.3 77.4 %all-to-all-done.5 = f32[3,2,2,512,256]{4,2,0,1,3:T(2,128)} async-done(((f32[3,2,2,512,256]{4,2,0,1,3:T(2,128)}), f32[3,2,2,512,256]{4,2,0,1,3:T(2,128)}, u32[]{:S(2)}, u32[]{:S(2)}) %all-to-all-start.5) | async-done | bytes 6291488 | tf_op jit(solution)/shard_map/all_to_all | solution.py:109
  383.7 4.3 all-to-all-start
  388.0 6.6 %copy.54 = f32[3,2,2,512,256]{4,3,2,1,0:T(8,128)} copy(f32[3,2,2,512,256]{4,2,0,1,3:T(2,128)} %all-to-all-done.5) | data formatting | bytes 12582912 | tf_op jit(solution)/shard_map/all_to_all | solution.py:109
  394.6 10.3 %copy.55 = f32[3,2,16,2,32,256]{5,3,2,4,0,1:T(2,128)} copy(f32[3,2,16,2,32,256]{5,4,2,3,1,0:T(8,128)} %bitcast.140) | data formatting | bytes 12582912 | tf_op jit(solution)/shard_map/all_to_all | solution.py:109
  404.9 8.5 %all_to_all.52 = f32[3,2,32,32,256]{4,2,3,0,1:T(8,128)} reshape(f32[3,2,16,2,32,256]{5,3,2,4,0,1:T(2,128)} %copy.55) | data formatting | bytes 12582912 | tf_op jit(solution)/shard_map/all_to_all | solution.py:109
  413.4 3.7 fusion
  417.1 0.0 copy-start.4
  417.1 4.9 %multiply_bitcast_fusion = f32[3,16,32,256]{3,1,2,0:T(8,128)} fusion(f32[3,32,256,16]{2,3,1,0:T(8,128)S(1)} %fusion, f32[3,2,32,32,256]{4,2,3,0,1:T(8,128)} %all_to_all.52, s32[32]{0:T(128)S(1)} %mul.319), kind=kOutput, calls=%fused_computation.34 | convolution fusion | flops 151788544 | bytes 6291584 | tf_op jit(solution)/shard_map/ik,skrc->sirc/dot_general | solution.py:15
  422.0 0.0 all-to-all-done
  422.0 0.0 copy-done.4
  422.0 1.8 fusion.36
  423.9 0.1 copy.56
  423.9 3.4 scatter_custom_fusion
  427.3 7.2 %all-to-all-start.6 = ((bf16[16,64,256]{2,1,0:T(8,128)(2,1)}), bf16[16,64,256]{2,1,0:T(8,128)(2,1)S(1)}, u32[]{:S(2)}, u32[]{:S(2)}) async-start(bf16[16,64,256]{2,1,0:T(8,128)(2,1)} %bitcast.44), calls=%async_computation.6 | async-start | bytes 1048576 | tf_op jit(solution)/shard_map/all_to_all | solution.py:129
  434.5 1.1 fusion.37
  435.6 1.1 copy.58
  436.7 0.8 copy.57
  437.5 7.1 %all-to-all-done.6 = bf16[16,64,256]{2,1,0:T(8,128)(2,1)S(1)} async-done(((bf16[16,64,256]{2,1,0:T(8,128)(2,1)}), bf16[16,64,256]{2,1,0:T(8,128)(2,1)S(1)}, u32[]{:S(2)}, u32[]{:S(2)}) %all-to-all-start.6) | async-done | bytes 524320 | tf_op jit(solution)/shard_map/all_to_all | solution.py:129
  444.6 0.8 copy.73
  445.4 0.0 copy-done.1
  (8 shorter events, 0.0 us)
Async XLA Ops:
  7.2 37.1 %copy-start = (bf16[256,4096]{1,0:T(8,128)(2,1)S(1)}, bf16[256,4096]{1,0:T(8,128)(2,1)}, u32[]{:S(2)}) copy-start(bf16[256,4096]{1,0:T(8,128)(2,1)} %param.13) | copy-start | bytes 6291460
  7.2 37.0 %all-gather.2.cloned.1.call-start = ((), (), s32[]{:S(2)}) async-start(), calls=%async_computation.7 | async-start | bytes 4718592 | tf_op jit(solution)/shard_map/all_gather | solution.py:50
  7.9 16.7 %all-to-all-start.1 = ((bf16[16,32,256]{2,1,0:T(8,128)(2,1)}), bf16[16,32,256]{2,1,0:T(8,128)(2,1)S(1)}, u32[]{:S(2)}, u32[]{:S(2)}) async-start(bf16[16,32,256]{2,1,0:T(8,128)(2,1)} %bitcast.142), calls=%async_computation.1 | async-start | bytes 524288 | tf_op jit(solution)/shard_map/all_to_all | solution.py:59
  24.6 23.9 %all-to-all-start.2 = ((bf16[16,32,256]{2,1,0:T(8,128)(2,1)}), bf16[16,32,256]{2,1,0:T(8,128)(2,1)S(1)}, u32[]{:S(2)}, u32[]{:S(2)}) async-start(bf16[16,32,256]{2,1,0:T(8,128)(2,1)} %bitcast.143), calls=%async_computation.2 | async-start | bytes 524288 | tf_op jit(solution)/shard_map/all_to_all | solution.py:62
  48.5 16.1 %all-to-all-start.3 = ((bf16[16,32,256]{2,1,0:T(8,128)(2,1)}), bf16[16,32,256]{2,1,0:T(8,128)(2,1)S(1)}, u32[]{:S(2)}, u32[]{:S(2)}) async-start(bf16[16,32,256]{2,1,0:T(8,128)(2,1)} %bitcast.5), calls=%async_computation.3 | async-start | bytes 524288 | tf_op jit(solution)/shard_map/all_to_all | solution.py:65
  78.5 102.5 %all-to-all-start.4 = ((f32[3,2,32,32,256]{4,3,0,1,2:T(8,128)}), f32[3,2,32,32,256]{4,3,0,1,2:T(8,128)}, u32[]{:S(2)}, u32[]{:S(2)}) async-start(f32[3,2,32,32,256]{4,3,0,1,2:T(8,128)} %copy.48), calls=%async_computation.4 | async-start | bytes 12582912 | tf_op jit(solution)/shard_map/all_to_all | solution.py:82
  297.1 9.0 %copy-start.2 = (s32[16,32]{1,0:T(8,128)S(1)}, s32[16,32]{1,0:T(8,128)}, u32[]{:S(2)}) copy-start(s32[16,32]{1,0:T(8,128)} %param.15) | copy-start | bytes 6148
  297.1 9.1 %copy-start.3 = (s32[16,32]{1,0:T(8,128)S(1)}, s32[16,32]{1,0:T(8,128)}, u32[]{:S(2)}) copy-start(s32[16,32]{1,0:T(8,128)} %param.14) | copy-start | bytes 6148
  297.1 86.5 %all-to-all-start.5 = ((f32[3,2,2,512,256]{4,2,0,1,3:T(2,128)}), f32[3,2,2,512,256]{4,2,0,1,3:T(2,128)}, u32[]{:S(2)}, u32[]{:S(2)}) async-start(f32[3,2,2,512,256]{4,2,0,1,3:T(2,128)} %copy.53), calls=%async_computation.5 | async-start | bytes 12582912 | tf_op jit(solution)/shard_map/all_to_all | solution.py:109
  383.7 38.3 %all-to-all-start = ((bf16[16,32,256]{2,1,0:T(8,128)(2,1)}), bf16[16,32,256]{2,1,0:T(8,128)(2,1)S(1)}, u32[]{:S(2)}, u32[]{:S(2)}) async-start(bf16[16,32,256]{2,1,0:T(8,128)(2,1)} %bitcast), calls=%async_computation | async-start | bytes 524288 | tf_op jit(solution)/shard_map/all_to_all | solution.py:68
  417.1 4.9 %copy-start.4 = (f32[256]{0:T(256)S(1)}, f32[256]{0:T(256)}, u32[]{:S(2)}) copy-start(f32[256]{0:T(256)} %param.11) | copy-start | bytes 3076
  422.0 23.4 %copy-start.1 = (bf16[256,4096]{1,0:T(8,128)(2,1)S(1)}, bf16[256,4096]{1,0:T(8,128)(2,1)}, u32[]{:S(2)}) copy-start(bf16[256,4096]{1,0:T(8,128)(2,1)} %param.13) | copy-start | bytes 6291460
  427.3 17.3 %all-to-all-start.6 = ((bf16[16,64,256]{2,1,0:T(8,128)(2,1)}), bf16[16,64,256]{2,1,0:T(8,128)(2,1)S(1)}, u32[]{:S(2)}, u32[]{:S(2)}) async-start(bf16[16,64,256]{2,1,0:T(8,128)(2,1)} %bitcast.44), calls=%async_computation.6 | async-start | bytes 1048576 | tf_op jit(solution)/shard_map/all_to_all | solution.py:129
Sparse Core Ops, SparseCore 0:
  9.7 34.4 all-gather.1
where the time goes:
time: 456 us; the launch traced here: 452 us
  waiting for transfers between devices  215 us (47%)
  matrix products  116 us (25%)
  local copies, waits for them, and re-layouts  52.1 us (11%)
  starting transfers between devices  44.4 us (10%)
  between operations  14.5 us (3%)
  other arithmetic  9.98 us (2%)
    dot_general x12, matrix products, contract(): return jnp.einsum(form, table, values, precision=exact_mode)  112 us
    all_to_all x1, waiting for transfers between devices, shards(): lax.all_to_all(turned, 'bins', split_axis=2, concat_axis=3, tiled=True)  97.4 us
    all_to_all x1, waiting for transfers between devices, shards(): lax.all_to_all(turned, 'bins', split_axis=3, concat_axis=2, tiled=True)  77.4 us
    all_to_all x3, local copies, waits for them, and re-layouts, shards(): lax.all_to_all(turned, 'bins', split_axis=3, concat_axis=2, tiled=True)  25.4 us
    all_gather x1, waiting for transfers between devices, shards(): lax.all_gather(out_grad, 'chan', axis=1, tiled=True)  16 us
    another operation x1, local copies, waits for them, and re-layouts, shards(): turned = jnp.stack([twist_re, twist_im], axis=1)  10.5 us
  transfers between devices with their start and end apart: 8, of which 6 were waited for; matrix products, arithmetic and copies ran while one was open for 7% of the time, Pallas kernels for 0%

commit v1 on v0

--- a/solution.py
+++ b/solution.py
@@ -47,7 +47,9 @@
     inner_cos = jnp.cos(inner_angle)
     inner_sin = jnp.sin(inner_angle)
     upstream = lax.dot_general(
-        lax.all_gather(out_grad, "chan", axis=1, tiled=True),
+        jnp.concatenate(
+            lax.all_to_all(jnp.stack([out_grad] * lax.axis_size("chan")), "chan", 0, 0), axis=1
+        ),
         out_weight,
         (((1,), (1,)), ((), ())),
         preferred_element_type=jnp.float32,

time: 456 us -> 463 us (1.015)
  between operations: 14.5 us -> 1.18 us
  waiting for transfers between devices: 215 us -> 228 us
    all_to_all x0 -> x1, waiting for transfers between devices: none -> 49.3 us  [shards(): lax.all_to_all(jnp.stack([out_grad] * lax.axis_size('chan')), 'chan', 0, 0)]
    all_to_all x1, waiting for transfers between devices: 97.4 us -> 77.7 us  [shards(): lax.all_to_all(turned, 'bins', split_axis=2, concat_axis=3, tiled=True)]
    all_gather x1 -> x0, waiting for transfers between devices: 16 us -> none  [shards(): lax.all_gather(out_grad, 'chan', axis=1, tiled=True)]
    all_to_all x0 -> x1, starting transfers between devices: none -> 4.7 us  [shards(): lax.all_to_all(jnp.stack([out_grad] * lax.axis_size('chan')), 'chan', 0, 0)]
  transfers between devices with their start and end apart: 8 -> 8, of which waited for: 6 -> 7; matrix products, arithmetic and copies ran while one was open for 7% -> 8% of each run, Pallas kernels for 0% -> 0%
where the time goes in v1:
time: 463 us; the launch traced here: 458 us
  waiting for transfers between devices  228 us (49%)
  matrix products  116 us (25%)
  local copies, waits for them, and re-layouts  55.8 us (12%)
  starting transfers between devices  47.3 us (10%)
  other arithmetic  9.97 us (2%)
    dot_general x12, matrix products, contract(): return jnp.einsum(form, table, values, precision=exact_mode)  112 us
    all_to_all x1, waiting for transfers between devices, shards(): lax.all_to_all(turned, 'bins', split_axis=2, concat_axis=3, tiled=True)  77.7 us
    all_to_all x1, waiting for transfers between devices, shards(): lax.all_to_all(turned, 'bins', split_axis=3, concat_axis=2, tiled=True)  73.9 us
    all_to_all x1, waiting for transfers between devices, shards(): lax.all_to_all(jnp.stack([out_grad] * lax.axis_size('chan')), 'chan', 0, 0)  49.3 us
    all_to_all x3, local copies, waits for them, and re-layouts, shards(): lax.all_to_all(turned, 'bins', split_axis=3, concat_axis=2, tiled=True)  25.4 us
    another operation x1, local copies, waits for them, and re-layouts, shards(): turned = jnp.stack([twist_re, twist_im], axis=1)  10.5 us
  transfers between devices with their start and end apart: 8, of which 7 were waited for; matrix products, arithmetic and copies ran while one was open for 8% of the time, Pallas kernels for 0%

profile of v1, /device:TPU:0, one launch (start us, length us, event | category | flops | bytes accessed | tf_op | source)
XLA Modules:
  0.0 458.0 jit_solution(4435090065130905610)
XLA Ops:
  0.6 0.0 copy-start
  0.6 8.3 %all-to-all-start.2 = ((bf16[16,32,256]{2,1,0:T(8,128)(2,1)}), bf16[16,32,256]{2,1,0:T(8,128)(2,1)S(1)}, u32[]{:S(2)}, u32[]{:S(2)}) async-start(bf16[16,32,256]{2,1,0:T(8,128)(2,1)} %bitcast.145), calls=%async_computation.2 | async-start | bytes 524288 | tf_op jit(solution)/shard_map/all_to_all | solution.py:61
  9.0 1.3 copy.45
  10.2 7.3 %all-to-all-done.2 = bf16[16,32,256]{2,1,0:T(8,128)(2,1)S(1)} async-done(((bf16[16,32,256]{2,1,0:T(8,128)(2,1)}), bf16[16,32,256]{2,1,0:T(8,128)(2,1)S(1)}, u32[]{:S(2)}, u32[]{:S(2)}) %all-to-all-start.2) | async-done | bytes 262176 | tf_op jit(solution)/shard_map/all_to_all | solution.py:61
  17.5 2.4 stack.61
  19.9 4.7 %all-to-all-start = ((bf16[8,512,512]{1,2,0:T(8,128)(2,1)}), bf16[8,512,512]{1,2,0:T(8,128)(2,1)}, u32[]{:S(2)}, u32[]{:S(2)}) async-start(bf16[8,512,512]{1,2,0:T(8,128)(2,1)} %stack.61), calls=%async_computation | async-start | bytes 8388608 | tf_op jit(solution)/shard_map/all_to_all | solution.py:51
  24.6 0.1 copy.50
  24.7 0.1 mul.319
  24.8 0.2 fusion.61
  25.0 49.3 %all-to-all-done = bf16[8,512,512]{1,2,0:T(8,128)(2,1)} async-done(((bf16[8,512,512]{1,2,0:T(8,128)(2,1)}), bf16[8,512,512]{1,2,0:T(8,128)(2,1)}, u32[]{:S(2)}, u32[]{:S(2)}) %all-to-all-start) | async-done | bytes 4194336 | tf_op jit(solution)/shard_map/all_to_all | solution.py:51
  74.2 3.6 all-to-all-start.3
  77.8 0.0 copy-done
  77.9 0.0 copy-done.5
  77.9 4.3 multiply_convert_fusion
  82.1 4.2 all-to-all-done.3
  86.4 3.8 all-to-all-start.4
  90.2 0.2 convert_bitcast_fusion.1
  90.3 0.2 bitcast_convert_fusion
  90.5 8.1 %all-to-all-done.4 = bf16[16,32,256]{2,1,0:T(8,128)(2,1)S(1)} async-done(((bf16[16,32,256]{2,1,0:T(8,128)(2,1)}), bf16[16,32,256]{2,1,0:T(8,128)(2,1)S(1)}, u32[]{:S(2)}, u32[]{:S(2)}) %all-to-all-start.4) | async-done | bytes 262176 | tf_op jit(solution)/shard_map/all_to_all | solution.py:67
  98.6 0.2 convert_bitcast_fusion
  98.8 2.8 fusion.16
  101.6 3.6 fusion.3
  105.2 1.1 pad_maximum_fusion
  106.3 6.3 %copy.51 = f32[3,2,32,32,256]{4,3,0,1,2:T(8,128)} copy(f32[3,2,32,32,256]{4,2,3,0,1:T(8,128)S(1)} %pad_maximum_fusion) | data formatting | bytes 12582912 | tf_op jit(solution)/shard_map/stack | solution.py:80
  112.6 4.9 %all-to-all-start.5 = ((f32[3,2,32,32,256]{4,3,0,1,2:T(8,128)}), f32[3,2,32,32,256]{4,3,0,1,2:T(8,128)}, u32[]{:S(2)}, u32[]{:S(2)}) async-start(f32[3,2,32,32,256]{4,3,0,1,2:T(8,128)} %copy.51), calls=%async_computation.5 | async-start | bytes 12582912 | tf_op jit(solution)/shard_map/all_to_all | solution.py:84
  117.5 0.1 dynamic_slice.3
  117.5 0.2 fusion.75
  117.7 77.7 %all-to-all-done.5 = f32[3,2,32,32,256]{4,3,0,1,2:T(8,128)} async-done(((f32[3,2,32,32,256]{4,3,0,1,2:T(8,128)}), f32[3,2,32,32,256]{4,3,0,1,2:T(8,128)}, u32[]{:S(2)}, u32[]{:S(2)}) %all-to-all-start.5) | async-done | bytes 6291488 | tf_op jit(solution)/shard_map/all_to_all | solution.py:84
  195.4 3.5 copy.53
  198.9 14.7 %fusion.7 = f32[3,2,256,512]{3,2,1,0:T(8,128)S(1)} fusion(f32[3,2,2,512,256]{4,3,2,1,0:T(8,128)S(1)} %bitcast.139), kind=kOutput, calls=%fused_computation.24 | convolution fusion | flops 4835508224 | bytes 6291456 | tf_op jit(solution)/shard_map/kr,slrc->slkc/dot_general | solution.py:15
  213.6 14.5 %fusion.6 = f32[3,2,256,512]{3,2,1,0:T(8,128)S(1)} fusion(f32[3,2,2,512,256]{4,3,2,1,0:T(8,128)S(1)} %bitcast.140), kind=kOutput, calls=%fused_computation.23 | convolution fusion | flops 4835508224 | bytes 6291456 | tf_op jit(solution)/shard_map/kr,slrc->slkc/dot_general | solution.py:15
  228.2 14.6 %add_bitcast_fusion.1 = f32[3,2,512,256]{2,3,1,0:T(8,128)S(1)} fusion(f32[3,2,256,512]{3,2,1,0:T(8,128)S(1)} %fusion.7, f32[3,2,2,512,256]{4,3,2,1,0:T(8,128)S(1)} %bitcast.141), kind=kOutput, calls=%fused_computation.22 | convolution fusion | flops 4836294656 | bytes 9437184 | tf_op jit(solution)/shard_map/kr,slrc->slkc/dot_general | solution.py:15
  242.8 14.5 %subtract_bitcast_fusion.1 = f32[3,2,512,256]{2,3,1,0:T(8,128)S(1)} fusion(f32[3,2,256,512]{3,2,1,0:T(8,128)S(1)} %fusion.6, f32[3,2,2,512,256]{4,3,2,1,0:T(8,128)S(1)} %bitcast.142), kind=kOutput, calls=%fused_computation.21 | convolution fusion | flops 4836294656 | bytes 9437184 | tf_op jit(solution)/shard_map/kr,slrc->slkc/dot_general | solution.py:15
  257.3 0.8 multiply_subtract_fusion.1
  258.1 0.8 multiply_subtract_fusion.2
  258.9 9.5 %fusion.10 = f32[3,2,256,512]{3,2,1,0:T(8,128)S(1)} fusion(f32[1,2,512,256]{2,3,1,0:T(8,128)S(1)} %get-tuple-element.22, f32[1,2,512,256]{2,3,1,0:T(8,128)S(1)} %get-tuple-element.21, f32[1,2,512,256]{2,3,1,0:T(8,128)S(1)} %get-tuple-element.24), kind=kOutput, calls=%fused_computation.27 | convolution fusion | flops 4837081088 | bytes 6291456 | tf_op jit(solution)/shard_map/rk,slkc->slrc/dot_general | solution.py:15
  268.3 9.4 %fusion.11 = f32[3,2,256,512]{3,2,1,0:T(8,128)S(1)} fusion(f32[1,2,512,256]{2,3,1,0:T(8,128)S(1)} %get-tuple-element.22, f32[1,2,512,256]{2,3,1,0:T(8,128)S(1)} %get-tuple-element.21, f32[1,2,512,256]{2,3,1,0:T(8,128)S(1)} %get-tuple-element.24), kind=kOutput, calls=%fused_computation.28 | convolution fusion | flops 4837081088 | bytes 6291456 | tf_op jit(solution)/shard_map/rk,slkc->slrc/dot_general | solution.py:15
  277.8 9.8 %fusion.14 = f32[3,2,256,512]{3,2,1,0:T(8,128)S(1)} fusion(f32[3,2,256,512]{3,2,1,0:T(8,128)S(1)} %fusion.11, f32[1,2,512,256]{2,3,1,0:T(8,128)S(1)} %get-tuple-element.20, f32[1,2,512,256]{2,3,1,0:T(8,128)S(1)} %get-tuple-element.23, f32[1,2,512,256]{2,3,1,0:T(8,128)S(1)} %get-tuple-element.19), kind=kOutput, calls=%fused_computation.31 | convolution fusion | flops 4837867520 | bytes 9437184 | tf_op jit(solution)/shard_map/rk,slkc->slrc/dot_general | solution.py:15
  287.6 9.9 %subtract_bitcast_fusion = (f32[3,1,2,512,256]{3,4,2,0,1:T(8,128)S(1)}, f32[3,1,2,512,256]{3,4,2,0,1:T(8,128)S(1)}) fusion(f32[3,2,256,512]{3,2,1,0:T(8,128)S(1)} %fusion.14, f32[2,512]{1,0:T(2,128)S(1)} %get-tuple-element.30, f32[2,512]{1,0:T(2,128)S(1)} %get-tuple-element.29, f32[3,2,256,512]{3,2,1,0:T(8,128)S(1)} %fusion.10, ...), kind=kOutput, calls=%fused_computation.20 | convolution fusion | flops 4842586112 | bytes 15736832 | tf_op jit(solution)/shard_map/rk,slkc->slrc/dot_general | solution.py:15
  297.5 3.5 pad_maximum_fusion.1
  301.0 10.5 %copy.56 = f32[3,2,2,512,256]{4,2,0,1,3:T(2,128)} copy(f32[3,2,2,512,256]{3,4,2,0,1:T(8,128)} %pad_maximum_fusion.1) | data formatting | bytes 12582912 | tf_op jit(solution)/shard_map/stack | solution.py:110
  311.5 8.4 %all-to-all-start.6 = ((f32[3,2,2,512,256]{4,2,0,1,3:T(2,128)}), f32[3,2,2,512,256]{4,2,0,1,3:T(2,128)}, u32[]{:S(2)}, u32[]{:S(2)}) async-start(f32[3,2,2,512,256]{4,2,0,1,3:T(2,128)} %copy.56), calls=%async_computation.6 | async-start | bytes 12582912 | tf_op jit(solution)/shard_map/all_to_all | solution.py:111
  319.9 0.0 copy-done.2
  319.9 0.0 copy-done.3
  320.0 0.1 sub.74
  320.0 73.9 %all-to-all-done.6 = f32[3,2,2,512,256]{4,2,0,1,3:T(2,128)} async-done(((f32[3,2,2,512,256]{4,2,0,1,3:T(2,128)}), f32[3,2,2,512,256]{4,2,0,1,3:T(2,128)}, u32[]{:S(2)}, u32[]{:S(2)}) %all-to-all-start.6) | async-done | bytes 6291488 | tf_op jit(solution)/shard_map/all_to_all | solution.py:111
  393.9 6.4 %all-to-all-start.1 = ((bf16[16,32,256]{2,1,0:T(8,128)(2,1)}), bf16[16,32,256]{2,1,0:T(8,128)(2,1)S(1)}, u32[]{:S(2)}, u32[]{:S(2)}) async-start(bf16[16,32,256]{2,1,0:T(8,128)(2,1)} %bitcast.2), calls=%async_computation.1 | async-start | bytes 524288 | tf_op jit(solution)/shard_map/all_to_all | solution.py:70
  400.3 6.6 %copy.57 = f32[3,2,2,512,256]{4,3,2,1,0:T(8,128)} copy(f32[3,2,2,512,256]{4,2,0,1,3:T(2,128)} %all-to-all-done.6) | data formatting | bytes 12582912 | tf_op jit(solution)/shard_map/all_to_all | solution.py:111
  406.9 10.3 %copy.58 = f32[3,2,16,2,32,256]{5,3,2,4,0,1:T(2,128)} copy(f32[3,2,16,2,32,256]{5,4,2,3,1,0:T(8,128)} %bitcast.143) | data formatting | bytes 12582912 | tf_op jit(solution)/shard_map/all_to_all | solution.py:111
  417.2 8.5 %all_to_all.56 = f32[3,2,32,32,256]{4,2,3,0,1:T(8,128)} reshape(f32[3,2,16,2,32,256]{5,3,2,4,0,1:T(2,128)} %copy.58) | data formatting | bytes 12582912 | tf_op jit(solution)/shard_map/all_to_all | solution.py:111
  425.7 3.7 fusion
  429.4 0.0 copy-start.4
  429.4 4.9 %multiply_bitcast_fusion = f32[3,16,32,256]{3,1,2,0:T(8,128)} fusion(f32[3,32,256,16]{2,3,1,0:T(8,128)S(1)} %fusion, f32[3,2,32,32,256]{4,2,3,0,1:T(8,128)} %all_to_all.56, s32[32]{0:T(128)S(1)} %mul.319), kind=kOutput, calls=%fused_computation.34 | convolution fusion | flops 151788544 | bytes 6291584 | tf_op jit(solution)/shard_map/ik,skrc->sirc/dot_general | solution.py:15
  434.3 0.0 all-to-all-done.1
  434.3 0.0 copy-done.4
  434.3 1.8 fusion.36
  436.2 0.1 copy.59
  436.3 3.4 scatter_custom_fusion
  439.6 7.2 %all-to-all-start.7 = ((bf16[16,64,256]{2,1,0:T(8,128)(2,1)}), bf16[16,64,256]{2,1,0:T(8,128)(2,1)S(1)}, u32[]{:S(2)}, u32[]{:S(2)}) async-start(bf16[16,64,256]{2,1,0:T(8,128)(2,1)} %bitcast.46), calls=%async_computation.7 | async-start | bytes 1048576 | tf_op jit(solution)/shard_map/all_to_all | solution.py:131
  446.8 1.1 fusion.37
  447.9 1.1 copy.61
  449.0 0.8 copy.60
  449.8 7.1 %all-to-all-done.7 = bf16[16,64,256]{2,1,0:T(8,128)(2,1)S(1)} async-done(((bf16[16,64,256]{2,1,0:T(8,128)(2,1)}), bf16[16,64,256]{2,1,0:T(8,128)(2,1)S(1)}, u32[]{:S(2)}, u32[]{:S(2)}) %all-to-all-start.7) | async-done | bytes 524320 | tf_op jit(solution)/shard_map/all_to_all | solution.py:131
  456.9 0.8 copy.76
  (11 shorter events, 0.0 us)
Async XLA Ops:
  0.6 77.2 %copy-start = (bf16[256,4096]{1,0:T(8,128)(2,1)S(1)}, bf16[256,4096]{1,0:T(8,128)(2,1)}, u32[]{:S(2)}) copy-start(bf16[256,4096]{1,0:T(8,128)(2,1)} %param.13) | copy-start | bytes 6291460
  0.6 16.8 %all-to-all-start.2 = ((bf16[16,32,256]{2,1,0:T(8,128)(2,1)}), bf16[16,32,256]{2,1,0:T(8,128)(2,1)S(1)}, u32[]{:S(2)}, u32[]{:S(2)}) async-start(bf16[16,32,256]{2,1,0:T(8,128)(2,1)} %bitcast.145), calls=%async_computation.2 | async-start | bytes 524288 | tf_op jit(solution)/shard_map/all_to_all | solution.py:61
  19.9 58.0 %copy-start.5 = (bf16[512,256]{1,0:T(8,128)(2,1)S(1)}, bf16[512,256]{1,0:T(8,128)(2,1)}, u32[]{:S(2)}) copy-start(bf16[512,256]{1,0:T(8,128)(2,1)} %param.10) | copy-start | bytes 786436
  19.9 54.3 %all-to-all-start = ((bf16[8,512,512]{1,2,0:T(8,128)(2,1)}), bf16[8,512,512]{1,2,0:T(8,128)(2,1)}, u32[]{:S(2)}, u32[]{:S(2)}) async-start(bf16[8,512,512]{1,2,0:T(8,128)(2,1)} %stack.61), calls=%async_computation | async-start | bytes 8388608 | tf_op jit(solution)/shard_map/all_to_all | solution.py:51
  74.2 12.1 %all-to-all-start.3 = ((bf16[16,32,256]{2,1,0:T(8,128)(2,1)}), bf16[16,32,256]{2,1,0:T(8,128)(2,1)S(1)}, u32[]{:S(2)}, u32[]{:S(2)}) async-start(bf16[16,32,256]{2,1,0:T(8,128)(2,1)} %bitcast.5), calls=%async_computation.3 | async-start | bytes 524288 | tf_op jit(solution)/shard_map/all_to_all | solution.py:64
  86.4 12.3 %all-to-all-start.4 = ((bf16[16,32,256]{2,1,0:T(8,128)(2,1)}), bf16[16,32,256]{2,1,0:T(8,128)(2,1)S(1)}, u32[]{:S(2)}, u32[]{:S(2)}) async-start(bf16[16,32,256]{2,1,0:T(8,128)(2,1)} %bitcast.7), calls=%async_computation.4 | async-start | bytes 524288 | tf_op jit(solution)/shard_map/all_to_all | solution.py:67
  112.6 82.8 %all-to-all-start.5 = ((f32[3,2,32,32,256]{4,3,0,1,2:T(8,128)}), f32[3,2,32,32,256]{4,3,0,1,2:T(8,128)}, u32[]{:S(2)}, u32[]{:S(2)}) async-start(f32[3,2,32,32,256]{4,3,0,1,2:T(8,128)} %copy.51), calls=%async_computation.5 | async-start | bytes 12582912 | tf_op jit(solution)/shard_map/all_to_all | solution.py:84
  311.5 8.4 %copy-start.2 = (s32[16,32]{1,0:T(8,128)S(1)}, s32[16,32]{1,0:T(8,128)}, u32[]{:S(2)}) copy-start(s32[16,32]{1,0:T(8,128)} %param.15) | copy-start | bytes 6148
  311.5 8.4 %copy-start.3 = (s32[16,32]{1,0:T(8,128)S(1)}, s32[16,32]{1,0:T(8,128)}, u32[]{:S(2)}) copy-start(s32[16,32]{1,0:T(8,128)} %param.14) | copy-start | bytes 6148
  311.5 82.4 %all-to-all-start.6 = ((f32[3,2,2,512,256]{4,2,0,1,3:T(2,128)}), f32[3,2,2,512,256]{4,2,0,1,3:T(2,128)}, u32[]{:S(2)}, u32[]{:S(2)}) async-start(f32[3,2,2,512,256]{4,2,0,1,3:T(2,128)} %copy.56), calls=%async_computation.6 | async-start | bytes 12582912 | tf_op jit(solution)/shard_map/all_to_all | solution.py:111
  393.9 40.4 %all-to-all-start.1 = ((bf16[16,32,256]{2,1,0:T(8,128)(2,1)}), bf16[16,32,256]{2,1,0:T(8,128)(2,1)S(1)}, u32[]{:S(2)}, u32[]{:S(2)}) async-start(bf16[16,32,256]{2,1,0:T(8,128)(2,1)} %bitcast.2), calls=%async_computation.1 | async-start | bytes 524288 | tf_op jit(solution)/shard_map/all_to_all | solution.py:70
  429.4 4.9 %copy-start.4 = (f32[256]{0:T(256)S(1)}, f32[256]{0:T(256)}, u32[]{:S(2)}) copy-start(f32[256]{0:T(256)} %param.11) | copy-start | bytes 3076
  434.3 23.4 %copy-start.1 = (bf16[256,4096]{1,0:T(8,128)(2,1)S(1)}, bf16[256,4096]{1,0:T(8,128)(2,1)}, u32[]{:S(2)}) copy-start(bf16[256,4096]{1,0:T(8,128)(2,1)} %param.13) | copy-start | bytes 6291460
  439.6 17.3 %all-to-all-start.7 = ((bf16[16,64,256]{2,1,0:T(8,128)(2,1)}), bf16[16,64,256]{2,1,0:T(8,128)(2,1)S(1)}, u32[]{:S(2)}, u32[]{:S(2)}) async-start(bf16[16,64,256]{2,1,0:T(8,128)(2,1)} %bitcast.46), calls=%async_computation.7 | async-start | bytes 1048576 | tf_op jit(solution)/shard_map/all_to_all | solution.py:131
